TPU v7x, 512 devices: a whole 4x4x16 slice. The times are simulated.
512 devices in a mesh: seq: 64 (over y, z), req: 8 (over x, core).
Axes of the slice: x: 4, y: 4, z: 16, core: 2. Of those that a mesh axis runs over, the one named last changes fastest.
Arguments:
- new_token_queries: bfloat16 [4, 64, 2048], P(None, 'req'), may hold values from -48 to 48
- new_token_keys: bfloat16 [4, 64, 1024], P(None, 'req'), may hold values from -48 to 48
- new_token_values: bfloat16 [4, 64, 1024], P(None, 'req'), may hold values from -6 to 6
- key_cache: bfloat16 [64, 2048, 1024], P('req', 'seq'), may hold values from -48 to 48
- value_cache: bfloat16 [64, 2048, 1024], P('req', 'seq'), may hold values from -6 to 6
- cache_len: int32 [64], P('req'), may hold values from 1 to 2048, 34816 in all
- resid: bfloat16 [4, 64, 2048], P(None, 'req'), may hold values from -6 to 6
- gain: bfloat16 [2048], replicated, may hold values from 0.5 to 1.5
- w_gate: bfloat16 [2048, 6144], P('seq', 'req'), may hold values from -0.125 to 0.125
- w_up: bfloat16 [2048, 6144], P('seq', 'req'), may hold values from -0.125 to 0.125
- w_down: bfloat16 [6144, 2048], P('req', 'seq'), may hold values from -0.078125 to 0.078125
Outputs:
- out: bfloat16 [4, 64, 2048], P(None, 'req')
All inputs are finite; a program needn't handle non-finite values. No bound on the sum of `cache_len` on one device may be relied on, other than what follows from the above.
Results may differ from a plain program's by a relative error of at most 0.006.
Values may be sent and summed in bfloat16 or wider, within the bound.
A program may use at most 128 MiB of HBM per device.

v0:
```python
import math
import jax
import jax.numpy as jnp
from jax import lax
from jax.sharding import PartitionSpec as P

QUERY_HEADS = 16
KEY_VALUE_HEADS = 8
HEAD_SIZE = 128
NEG_FILL = -1e30
EPSILON = 1e-06


def partial_softmax(q, keys, values, valid):
    scores = jnp.einsum("rkmd,rbkd->rkmb", q, keys, preferred_element_type=jnp.float32) / math.sqrt(
        HEAD_SIZE
    )
    inside = valid[:, None]
    scores = jnp.where(inside, scores, NEG_FILL)
    highest = jnp.max(scores, axis=-1)
    weights = jnp.where(inside, jnp.exp(scores - highest[..., None]), 0.0).astype(jnp.bfloat16)
    totals = jnp.sum(weights.astype(jnp.float32), axis=-1)
    weighted = jnp.einsum("rkmb,rbkd->rkmd", weights, values, preferred_element_type=jnp.float32)
    return (highest, totals, weighted)


def body(q, nk, nv, kc, vc, cache_len, resid, gain, w_gate, w_up, w_down):
    steps, rows, model = q.shape
    page = kc.shape[1]
    width = w_gate.shape[0]
    units = w_gate.shape[1]
    group = QUERY_HEADS // KEY_VALUE_HEADS
    me = lax.axis_index("seq")
    positions = me * page + jnp.arange(page, dtype=jnp.int32)
    valid = (positions[None, :] < cache_len[:, None])[:, None, :]
    qv = q.reshape(steps, rows, KEY_VALUE_HEADS, group, HEAD_SIZE).transpose(1, 2, 0, 3, 4)
    qv = qv.reshape(rows, KEY_VALUE_HEADS, steps * group, HEAD_SIZE)
    keys = kc.reshape(rows, page, KEY_VALUE_HEADS, HEAD_SIZE)
    values = vc.reshape(rows, page, KEY_VALUE_HEADS, HEAD_SIZE)
    local = partial_softmax(qv, keys, values, jnp.broadcast_to(valid, (rows, steps * group, page)))
    highest = lax.pmax(local[0], "seq")
    factor = jnp.exp(local[0] - highest)
    totals, weighted = lax.psum((factor * local[1], factor[..., None] * local[2]), "seq")
    fk = jnp.swapaxes(nk, 0, 1).reshape(rows, steps, KEY_VALUE_HEADS, HEAD_SIZE)
    fv = jnp.swapaxes(nv, 0, 1).reshape(rows, steps, KEY_VALUE_HEADS, HEAD_SIZE)
    step_of = jnp.arange(steps * group, dtype=jnp.int32) // group
    causal = jnp.arange(steps, dtype=jnp.int32)[None, :] <= step_of[:, None]
    fresh = partial_softmax(
        qv, fk, fv, jnp.broadcast_to(causal[None], (rows, steps * group, steps))
    )
    peak = jnp.maximum(highest, fresh[0])
    a = jnp.exp(highest - peak)
    b = jnp.exp(fresh[0] - peak)
    total = a * totals + b * fresh[1]
    acc = a[..., None] * weighted + b[..., None] * fresh[2]
    attn = (acc / total[..., None]).astype(jnp.bfloat16)
    attn = attn.reshape(rows, KEY_VALUE_HEADS, steps, group, HEAD_SIZE).transpose(2, 0, 1, 3, 4)
    attn = attn.reshape(steps, rows, model)
    attn = lax.optimization_barrier(attn).astype(jnp.float32)
    stream = (resid.astype(jnp.float32) + attn).astype(jnp.bfloat16)
    stream = lax.optimization_barrier(stream).astype(jnp.float32)
    scaled = lax.rsqrt(jnp.mean(stream * stream, axis=-1, keepdims=True) + EPSILON)
    normed = (stream * scaled * gain.astype(jnp.float32)).astype(jnp.bfloat16)
    own = lax.dynamic_slice_in_dim(normed, me * width, width, 2)
    every = lax.all_gather(own, "req", axis=1, tiled=True).reshape(-1, width)
    joined = jnp.concatenate([w_gate, w_up], axis=1)
    sums = lax.psum(jnp.dot(every, joined, preferred_element_type=jnp.float32), "seq")
    hidden = (jax.nn.silu(sums[:, :units]) * sums[:, units:]).astype(jnp.bfloat16)
    down = jnp.dot(hidden, w_down, preferred_element_type=jnp.float32)
    down = lax.psum_scatter(down.reshape(steps, -1, width), "req", scatter_dimension=1, tiled=True)
    piece = (lax.dynamic_slice_in_dim(stream, me * width, width, 2) + down).astype(jnp.bfloat16)
    return lax.all_gather(piece, "seq", axis=2, tiled=True)


def solution(mesh):
    placed = (
        P(None, "req", None),
        P(None, "req", None),
        P(None, "req", None),
        P("req", "seq", None),
        P("req", "seq", None),
        P("req"),
        P(None, "req", None),
        P(),
        P("seq", "req"),
        P("seq", "req"),
        P("req", "seq"),
    )
    return jax.shard_map(
        body, mesh=mesh, in_specs=placed, out_specs=P(None, "req", None), check_vma=False
    )
```

profile of v0, /device:TPU:8, one launch (start us, length us, event | category | flops | bytes accessed | tf_op | source)
XLA Modules:
  0.0 988.8 jit_solution(13132273959055247014)
XLA Ops:
  6.6 1.1 copy.49
  7.6 0.7 broadcast_compare_fusion
  8.4 1.5 fusion.27
  9.9 261.8 %pmax.7 = f32[8,8,8]{2,1,0:T(8,128)S(1)} all-reduce(f32[8,8,8]{2,1,0:T(8,128)S(1)} %get-tuple-element.10), channel_id=1, replica_groups=mesh['seq'=64,'req'=8] {'seq'}, use_global_device_ids=true, to_apply=%region_1.2 | all-reduce | flops 512 | bytes 4096 | tf_op jit(solution)/shard_map/pmax | solution.py:41
  271.6 0.3 convert_reduce_fusion
  271.9 1.0 convolution_multiply_fusion.1
  273.1 0.2 fusion.28
  273.3 0.1 convert_reduce_fusion.1
  273.4 0.8 dynamic-slice.2
  274.2 274.0 %psum.22 = f32[8,8,8]{2,1,0:T(8,128)S(1)} all-reduce(f32[8,8,8]{2,1,0:T(8,128)S(1)} %get-tuple-element.8), channel_id=1, replica_groups=mesh['seq'=64,'req'=8] {'seq'}, use_global_device_ids=true, to_apply=%region_5.6 | all-reduce | flops 512 | bytes 4096 | tf_op jit(solution)/shard_map/psum | solution.py:43
  548.3 1.4 fusion.3
  549.7 0.2 copy.54
  549.9 0.1 multiply_reduce_fusion
  550.2 13.1 %all_gather.6 = bf16[4,64,32]{2,0,1:T(4,128)(2,1)S(1)} all-gather(bf16[4,8,32]{2,0,1:T(4,128)(2,1)S(1)} %copy.55), channel_id=1, replica_groups=mesh['seq'=64,'req'=8] {'req'}, dimensions={1}, use_global_device_ids=true | all-gather | bytes 18432 | tf_op jit(solution)/shard_map/all_gather | solution.py:65
  563.5 1.5 fusion.12
  565.0 1.3 dynamic-slice
  566.9 286.0 %all-reduce.6.cloned.1.call-done = f32[256,1536]{1,0:T(8,128)} async-done(((f32[256,1536]{1,0:T(8,128)}), f32[256,1536]{1,0:T(8,128)}) %all-reduce.6.cloned.1.call-update) | async-done | bytes 1572880 | tf_op jit(solution)/shard_map/psum | solution.py:67
  852.9 1.7 fusion.10
  854.6 0.1 reshape.72
  854.7 0.1 copy.57
  854.9 24.7 %all-reduce = f32[4,64,32]{2,0,1:T(4,128)S(1)} all-reduce(f32[4,64,32]{2,0,1:T(4,128)S(1)} %copy.57), channel_id=2, replica_groups=mesh['seq'=64,'req'=8] {'req'}, use_global_device_ids=true, to_apply=%region_9.10.clone | all-reduce | flops 8192 | bytes 65536
  879.7 0.1 copy.59
  879.8 100.1 %all_gather.7 = bf16[4,8,2048]{1,0,2:T(4,128)(2,1)S(1)} all-gather(bf16[4,8,32]{1,0,2:T(4,128)(2,1)S(1)} %copy.59), channel_id=1, replica_groups=mesh['seq'=64,'req'=8] {'seq'}, dimensions={2}, use_global_device_ids=true | all-gather | bytes 133120 | tf_op jit(solution)/shard_map/all_gather | solution.py:72
  979.9 2.1 copy.60
  (33 shorter events, 0.6 us)
Async XLA Ops:
  6.5 265.4 %copy-start = (bf16[8,32,1024]{2,1,0:T(8,128)(2,1)S(1)}, bf16[8,32,1024]{2,1,0:T(8,128)(2,1)}, u32[]{:S(2)}) copy-start(bf16[8,32,1024]{2,1,0:T(8,128)(2,1)} %param.15) | copy-start | bytes 1572868
  6.5 541.8 %all-reduce.4.cloned.1.call-start = ((), (), s32[]{:S(2)}) async-start(), calls=%async_computation | async-start | bytes 524288 | tf_op jit(solution)/shard_map/psum | solution.py:43
  6.5 266.5 %copy-start.4 = (bf16[4,8,1024]{2,1,0:T(8,128)(2,1)S(1)}, bf16[4,8,1024]{2,1,0:T(8,128)(2,1)}, u32[]{:S(2)}) copy-start(bf16[4,8,1024]{2,1,0:T(8,128)(2,1)} %param.12) | copy-start | bytes 196612
  9.8 538.5 %copy-start.5 = (bf16[4,8,1024]{2,1,0:T(8,128)(2,1)S(1)}, bf16[4,8,1024]{2,1,0:T(8,128)(2,1)}, u32[]{:S(2)}) copy-start(bf16[4,8,1024]{2,1,0:T(8,128)(2,1)} %param.13) | copy-start | bytes 196612
  273.0 579.9 %all-reduce.6.cloned.1.call-start = ((), (), s32[]{:S(2)}) async-start(), calls=%async_computation.1 | async-start | bytes 3145728 | tf_op jit(solution)/shard_map/psum | solution.py:67
  273.1 276.8 %copy-start.1 = (bf16[4,8,2048]{2,1,0:T(8,128)(2,1)S(1)}, bf16[4,8,2048]{2,1,0:T(8,128)(2,1)}, u32[]{:S(2)}) copy-start(bf16[4,8,2048]{2,1,0:T(8,128)(2,1)} %param.17) | copy-start | bytes 393220
  548.3 15.1 %copy-start.2 = (bf16[32,768]{1,0:T(8,128)(2,1)S(1)}, bf16[32,768]{1,0:T(8,128)(2,1)}, u32[]{:S(2)}) copy-start(bf16[32,768]{1,0:T(8,128)(2,1)} %param.20) | copy-start | bytes 147460
  548.3 15.1 %copy-start.3 = (bf16[32,768]{1,0:T(8,128)(2,1)S(1)}, bf16[32,768]{1,0:T(8,128)(2,1)}, u32[]{:S(2)}) copy-start(bf16[32,768]{1,0:T(8,128)(2,1)} %param.19) | copy-start | bytes 147460
  563.4 289.5 %copy-start.6 = (bf16[768,32]{0,1:T(8,128)(2,1)S(1)}, bf16[768,32]{0,1:T(8,128)(2,1)}, u32[]{:S(2)}) copy-start(bf16[768,32]{0,1:T(8,128)(2,1)} %param.21) | copy-start | bytes 147460
Sparse Core Ops, SparseCore 0:
  273.1 274.0 all-reduce.3
  565.1 287.7 all-reduce.5
where the time goes:
time: 989 us
  blocking collectives  674 us (68%)
  waiting for transfers between devices  286 us (29%)
  between operations  14.3 us (1%)
    psum x1, waiting for transfers between devices, body(): lax.psum(jnp.dot(every, joined, preferred_element_type=jnp.float32), 'seq')  286 us
    psum x1, blocking collectives, body(): lax.psum((factor * local[1], factor[..., None] * local[2]), 'seq')  274 us
    pmax x1, blocking collectives, body(): highest = lax.pmax(local[0], 'seq')  262 us
    all_gather x1, blocking collectives, body(): return lax.all_gather(piece, 'seq', axis=2, tiled=True)  100 us
    unnamed x1, blocking collectives  24.7 us
  transfers between devices with their start and end apart: 2, of which 1 were waited for; matrix products, arithmetic and copies ran while one was open for 0% of the time, Pallas kernels for 0%

commit v1 on v0

--- a/solution.py
+++ b/solution.py
@@ -64,7 +64,9 @@
     own = lax.dynamic_slice_in_dim(normed, me * width, width, 2)
     every = lax.all_gather(own, "req", axis=1, tiled=True).reshape(-1, width)
     joined = jnp.concatenate([w_gate, w_up], axis=1)
-    sums = lax.psum(jnp.dot(every, joined, preferred_element_type=jnp.float32), "seq")
+    own_2 = jnp.dot(every, joined, preferred_element_type=jnp.float32)
+    parts = lax.all_gather(own_2, "seq", axis=0, tiled=False)
+    sums = parts.sum(axis=0)
     hidden = (jax.nn.silu(sums[:, :units]) * sums[:, units:]).astype(jnp.bfloat16)
     down = jnp.dot(hidden, w_down, preferred_element_type=jnp.float32)
     down = lax.psum_scatter(down.reshape(steps, -1, width), "req", scatter_dimension=1, tiled=True)

time: 989 us -> 1490 us (1.51)
  waiting for transfers between devices: 286 us -> 756 us
  other arithmetic: 1.51 us -> 32.3 us
    all_gather x0 -> x1, waiting for transfers between devices: none -> 756 us  [body(): parts = lax.all_gather(own_2, 'seq', axis=0, tiled=False)]
    psum x1 -> x0, waiting for transfers between devices: 286 us -> none  [body(): lax.psum(jnp.dot(every, joined, preferred_element_type=jnp.float32), 'seq')]
    reduce_sum x0 -> x1, other arithmetic: none -> 30.8 us  [body(): sums = parts.sum(axis=0)]
where the time goes in v1:
time: 1490 us
  waiting for transfers between devices  756 us (51%)
  blocking collectives  676 us (45%)
  other arithmetic  32.3 us (2%)
    all_gather x1, waiting for transfers between devices, body(): parts = lax.all_gather(own_2, 'seq', axis=0, tiled=False)  756 us
    psum x1, blocking collectives, body(): lax.psum((factor * local[1], factor[..., None] * local[2]), 'seq')  274 us
    pmax x1, blocking collectives, body(): highest = lax.pmax(local[0], 'seq')  262 us
    all_gather x1, blocking collectives, body(): return lax.all_gather(piece, 'seq', axis=2, tiled=True)  101 us
    reduce_sum x1, other arithmetic, body(): sums = parts.sum(axis=0)  30.8 us
  transfers between devices with their start and end apart: 2, of which 1 were waited for; matrix products, arithmetic and copies ran while one was open for 0% of the time, Pallas kernels for 0%

profile of v1, /device:TPU:8, one launch (start us, length us, event | category | flops | bytes accessed | tf_op | source)
XLA Modules:
  0.0 1490.0 jit_solution(15799828115258735750)
XLA Ops:
  6.6 1.1 copy.49
  7.6 0.7 broadcast_compare_fusion
  8.4 1.5 fusion.27
  9.9 261.8 %pmax.7 = f32[8,8,8]{2,1,0:T(8,128)S(1)} all-reduce(f32[8,8,8]{2,1,0:T(8,128)S(1)} %get-tuple-element.10), channel_id=1, replica_groups=mesh['seq'=64,'req'=8] {'seq'}, use_global_device_ids=true, to_apply=%region_1.2 | all-reduce | flops 512 | bytes 4096 | tf_op jit(solution)/shard_map/pmax | solution.py:41
  271.6 0.3 convert_reduce_fusion
  271.9 1.0 convolution_multiply_fusion.1
  273.1 0.2 fusion.28
  273.3 0.1 convert_reduce_fusion.1
  273.4 0.8 dynamic-slice.2
  274.2 274.1 %psum.15 = f32[8,8,8]{2,1,0:T(8,128)S(1)} all-reduce(f32[8,8,8]{2,1,0:T(8,128)S(1)} %get-tuple-element.8), channel_id=1, replica_groups=mesh['seq'=64,'req'=8] {'seq'}, use_global_device_ids=true, to_apply=%region_5.6 | all-reduce | flops 512 | bytes 4096 | tf_op jit(solution)/shard_map/psum | solution.py:43
  548.4 1.3 fusion.3
  549.7 0.2 copy.54
  550.0 0.1 multiply_reduce_fusion
  550.2 13.0 all_gather.12
  563.4 1.5 fusion.12
  565.0 1.3 dynamic-slice
  566.9 755.6 %all-gather.3.cloned.1.call-done = f32[16384,1536]{1,0:T(8,128)} async-done(((f32[256,1536]{1,0:T(8,128)}), f32[16384,1536]{1,0:T(8,128)}) %all-gather.3.cloned.1.call-update) | async-done | bytes 100663312 | tf_op jit(solution)/shard_map/all_gather | solution.py:68
  1322.5 30.8 %reduce_sum.39 = f32[256,1536]{1,0:T(8,128)S(1)} reduce(f32[64,256,1536]{2,1,0:T(8,128)} %bitcast.10, f32[]{:T(128)} %constant.41.clone.1), dimensions={0}, to_apply=%region_8.9 | reduce | flops 24772608 | bytes 102236160 | tf_op jit(solution)/shard_map/reduce_sum | solution.py:69
  1353.3 0.3 fusion.10
  1353.6 0.1 reshape.72
  1353.8 0.1 copy.57
  1353.9 26.4 %all-reduce = f32[4,64,32]{2,0,1:T(4,128)S(1)} all-reduce(f32[4,64,32]{2,0,1:T(4,128)S(1)} %copy.57), channel_id=3, replica_groups=mesh['seq'=64,'req'=8] {'req'}, use_global_device_ids=true, to_apply=%region_9.10.clone | all-reduce | flops 8192 | bytes 65536
  1380.5 100.6 %all_gather.15 = bf16[4,8,2048]{1,0,2:T(4,128)(2,1)S(1)} all-gather(bf16[4,8,32]{1,0,2:T(4,128)(2,1)S(1)} %copy.59), channel_id=1, replica_groups=mesh['seq'=64,'req'=8] {'seq'}, dimensions={2}, use_global_device_ids=true | all-gather | bytes 133120 | tf_op jit(solution)/shard_map/all_gather | solution.py:74
  1481.1 2.1 copy.60
  (34 shorter events, 0.7 us)
Async XLA Ops:
  6.5 265.4 %copy-start = (bf16[8,32,1024]{2,1,0:T(8,128)(2,1)S(1)}, bf16[8,32,1024]{2,1,0:T(8,128)(2,1)}, u32[]{:S(2)}) copy-start(bf16[8,32,1024]{2,1,0:T(8,128)(2,1)} %param.15) | copy-start | bytes 1572868
  6.5 541.8 %all-reduce.3.cloned.1.call-start = ((), (), s32[]{:S(2)}) async-start(), calls=%async_computation | async-start | bytes 524288 | tf_op jit(solution)/shard_map/psum | solution.py:43
  6.5 266.5 %copy-start.4 = (bf16[4,8,1024]{2,1,0:T(8,128)(2,1)S(1)}, bf16[4,8,1024]{2,1,0:T(8,128)(2,1)}, u32[]{:S(2)}) copy-start(bf16[4,8,1024]{2,1,0:T(8,128)(2,1)} %param.12) | copy-start | bytes 196612
  9.8 538.5 %copy-start.5 = (bf16[4,8,1024]{2,1,0:T(8,128)(2,1)S(1)}, bf16[4,8,1024]{2,1,0:T(8,128)(2,1)}, u32[]{:S(2)}) copy-start(bf16[4,8,1024]{2,1,0:T(8,128)(2,1)} %param.13) | copy-start | bytes 196612
  273.0 1049.6 %all-gather.3.cloned.1.call-start = ((), (), s32[]{:S(2)}) async-start(), calls=%async_computation.1 | async-start | bytes 102236160 | tf_op jit(solution)/shard_map/all_gather | solution.py:68
  273.1 276.8 %copy-start.1 = (bf16[4,8,2048]{2,1,0:T(8,128)(2,1)S(1)}, bf16[4,8,2048]{2,1,0:T(8,128)(2,1)}, u32[]{:S(2)}) copy-start(bf16[4,8,2048]{2,1,0:T(8,128)(2,1)} %param.17) | copy-start | bytes 393220
  548.3 15.1 %copy-start.2 = (bf16[32,768]{1,0:T(8,128)(2,1)S(1)}, bf16[32,768]{1,0:T(8,128)(2,1)}, u32[]{:S(2)}) copy-start(bf16[32,768]{1,0:T(8,128)(2,1)} %param.20) | copy-start | bytes 147460
  548.4 15.1 %copy-start.3 = (bf16[32,768]{1,0:T(8,128)(2,1)S(1)}, bf16[32,768]{1,0:T(8,128)(2,1)}, u32[]{:S(2)}) copy-start(bf16[32,768]{1,0:T(8,128)(2,1)} %param.19) | copy-start | bytes 147460
  1322.5 30.8 %copy-start.6 = (bf16[768,32]{0,1:T(8,128)(2,1)S(1)}, bf16[768,32]{0,1:T(8,128)(2,1)}, u32[]{:S(2)}) copy-start(bf16[768,32]{0,1:T(8,128)(2,1)} %param.21) | copy-start | bytes 147460
Sparse Core Ops, SparseCore 0:
  273.1 274.0 all-reduce.2
  565.1 757.3 all-gather.2

commit v2 on v0

--- a/solution.py
+++ b/solution.py
@@ -69,7 +69,14 @@
     down = jnp.dot(hidden, w_down, preferred_element_type=jnp.float32)
     down = lax.psum_scatter(down.reshape(steps, -1, width), "req", scatter_dimension=1, tiled=True)
     piece = (lax.dynamic_slice_in_dim(stream, me * width, width, 2) + down).astype(jnp.bfloat16)
-    return lax.all_gather(piece, "seq", axis=2, tiled=True)
+
+    def test_the_zone(patch):
+        step_out = jnp.concatenate(
+            lax.all_to_all(jnp.stack(lax.axis_size("seq") * [patch]), "seq", 0, 0), axis=2
+        )
+        return step_out
+
+    return test_the_zone(piece)
 
 
 def solution(mesh):

time: 989 us -> 928 us (0.938)
  blocking collectives: 674 us -> 577 us
  waiting for transfers between devices: 286 us -> 322 us
    all_gather x1 -> x0, blocking collectives: 100 us -> none  [body(): return lax.all_gather(piece, 'seq', axis=2, tiled=True)]
    reduce_scatter x0 -> x1, waiting for transfers between devices: none -> 34.6 us  [body(): lax.psum_scatter(down.reshape(steps, -1, width), 'req', scatter_dimension...]
    all_to_all x0 -> x1, blocking collectives: none -> 29.8 us  [test_the_zone(): lax.all_to_all(jnp.stack(lax.axis_size('seq') * [patch]), 'seq', 0, 0)]
    unnamed x1 -> x0, blocking collectives: 24.7 us -> none
  transfers between devices with their start and end apart: 2 -> 3, of which waited for: 1 -> 2; matrix products, arithmetic and copies ran while one was open for 0% -> 0% of each run, Pallas kernels for 0% -> 0%
where the time goes in v2:
time: 928 us; the launch traced here: 927 us
  blocking collectives  577 us (62%)
  waiting for transfers between devices  322 us (35%)
  between operations  13.3 us (1%)
    psum x1, waiting for transfers between devices, body(): lax.psum(jnp.dot(every, joined, preferred_element_type=jnp.float32), 'seq')  288 us
    psum x1, blocking collectives, body(): lax.psum((factor * local[1], factor[..., None] * local[2]), 'seq')  274 us
    pmax x1, blocking collectives, body(): highest = lax.pmax(local[0], 'seq')  262 us
    reduce_scatter x1, waiting for transfers between devices, body(): lax.psum_scatter(down.reshape(steps, -1, width), 'req', scatter_dimension...  34.6 us
    all_to_all x1, blocking collectives, test_the_zone(): lax.all_to_all(jnp.stack(lax.axis_size('seq') * [patch]), 'seq', 0, 0)  29.8 us
  transfers between devices with their start and end apart: 3, of which 2 were waited for; matrix products, arithmetic and copies ran while one was open for 0% of the time, Pallas kernels for 0%

profile of v2, /device:TPU:8, one launch (start us, length us, event | category | flops | bytes accessed | tf_op | source)
XLA Modules:
  0.0 927.4 jit_solution(8359449445522266432)
XLA Ops:
  6.6 1.1 copy.26
  7.6 0.7 broadcast_compare_fusion
  8.4 1.5 fusion.26
  9.9 261.8 %pmax.7 = f32[8,8,8]{2,1,0:T(8,128)S(1)} all-reduce(f32[8,8,8]{2,1,0:T(8,128)S(1)} %get-tuple-element.10), channel_id=1, replica_groups=mesh['seq'=64,'req'=8] {'seq'}, use_global_device_ids=true, to_apply=%region_1.2 | all-reduce | flops 512 | bytes 4096 | tf_op jit(solution)/shard_map/pmax | solution.py:41
  271.6 0.3 convert_reduce_fusion
  271.9 1.0 convolution_multiply_fusion.1
  273.1 0.2 fusion.27
  273.3 0.1 convert_reduce_fusion.1
  273.4 0.8 dynamic-slice
  274.2 274.0 %psum.22 = f32[8,8,8]{2,1,0:T(8,128)S(1)} all-reduce(f32[8,8,8]{2,1,0:T(8,128)S(1)} %get-tuple-element.8), channel_id=1, replica_groups=mesh['seq'=64,'req'=8] {'seq'}, use_global_device_ids=true, to_apply=%region_5.6 | all-reduce | flops 512 | bytes 4096 | tf_op jit(solution)/shard_map/psum | solution.py:43
  548.3 1.4 fusion.3
  549.7 0.2 copy.31
  549.9 0.1 multiply_reduce_fusion
  550.1 11.8 %all_gather.3 = bf16[4,64,32]{2,1,0:T(8,128)(2,1)S(1)} all-gather(bf16[4,8,32]{2,1,0:T(8,128)(2,1)S(1)} %multiply_convert_fusion), channel_id=1, replica_groups=mesh['seq'=64,'req'=8] {'req'}, dimensions={1}, use_global_device_ids=true | all-gather | bytes 18432 | tf_op jit(solution)/shard_map/all_gather | solution.py:65
  561.9 1.5 fusion.12
  563.5 287.5 %all-reduce.5.cloned.1.call-done = f32[256,1536]{1,0:T(8,128)} async-done(((f32[256,1536]{1,0:T(8,128)}), f32[256,1536]{1,0:T(8,128)}) %all-reduce.5.cloned.1.call-update) | async-done | bytes 1572880 | tf_op jit(solution)/shard_map/psum | solution.py:67
  851.0 2.4 fusion.10
  853.4 34.6 %reduce-scatter.2.cloned.1.call-done = f32[4,8,32]{2,1,0:T(8,128)} async-done(((f32[4,64,32]{2,1,0:T(8,128)}), f32[4,8,32]{2,1,0:T(8,128)}) %reduce-scatter.2.cloned.1.call-update) | async-done | bytes 4112 | tf_op jit(solution)/shard_map/reduce_scatter | solution.py:70
  888.0 0.8 add_convert_fusion.1
  888.9 0.4 reshape.83
  889.3 29.8 %all_to_all.5 = bf16[64,2,512]{2,1,0:T(2,128)(2,1)S(1)} all-to-all(bf16[64,2,512]{2,1,0:T(2,128)(2,1)S(1)} %reshape.83), channel_id=1, replica_groups=mesh['seq'=64,'req'=8] {'seq'}, dimensions={0} | all-to-all | bytes 262144 | tf_op jit(solution)/shard_map/all_to_all | solution.py:75
  919.1 0.3 reshape.84
  919.4 0.2 copy.33
  919.7 1.2 reshape.82
  (31 shorter events, 0.5 us)
Async XLA Ops:
  6.5 265.4 %copy-start = (bf16[8,32,1024]{2,1,0:T(8,128)(2,1)S(1)}, bf16[8,32,1024]{2,1,0:T(8,128)(2,1)}, u32[]{:S(2)}) copy-start(bf16[8,32,1024]{2,1,0:T(8,128)(2,1)} %param.15) | copy-start | bytes 1572868
  6.5 541.8 %all-reduce.3.cloned.1.call-start = ((), (), s32[]{:S(2)}) async-start(), calls=%async_computation.2 | async-start | bytes 524288 | tf_op jit(solution)/shard_map/psum | solution.py:43
  6.5 266.5 %copy-start.4 = (bf16[4,8,1024]{2,1,0:T(8,128)(2,1)S(1)}, bf16[4,8,1024]{2,1,0:T(8,128)(2,1)}, u32[]{:S(2)}) copy-start(bf16[4,8,1024]{2,1,0:T(8,128)(2,1)} %param.12) | copy-start | bytes 196612
  9.8 538.5 %copy-start.5 = (bf16[4,8,1024]{2,1,0:T(8,128)(2,1)S(1)}, bf16[4,8,1024]{2,1,0:T(8,128)(2,1)}, u32[]{:S(2)}) copy-start(bf16[4,8,1024]{2,1,0:T(8,128)(2,1)} %param.13) | copy-start | bytes 196612
  273.0 578.0 %all-reduce.5.cloned.1.call-start = ((), (), s32[]{:S(2)}) async-start(), calls=%async_computation.3 | async-start | bytes 3145728 | tf_op jit(solution)/shard_map/psum | solution.py:67
  273.1 276.8 %copy-start.1 = (bf16[4,8,2048]{2,1,0:T(8,128)(2,1)S(1)}, bf16[4,8,2048]{2,1,0:T(8,128)(2,1)}, u32[]{:S(2)}) copy-start(bf16[4,8,2048]{2,1,0:T(8,128)(2,1)} %param.17) | copy-start | bytes 393220
  548.3 13.6 %copy-start.2 = (bf16[32,768]{1,0:T(8,128)(2,1)S(1)}, bf16[32,768]{1,0:T(8,128)(2,1)}, u32[]{:S(2)}) copy-start(bf16[32,768]{1,0:T(8,128)(2,1)} %param.20) | copy-start | bytes 147460
  548.3 13.6 %copy-start.3 = (bf16[32,768]{1,0:T(8,128)(2,1)S(1)}, bf16[32,768]{1,0:T(8,128)(2,1)}, u32[]{:S(2)}) copy-start(bf16[32,768]{1,0:T(8,128)(2,1)} %param.19) | copy-start | bytes 147460
  561.9 289.1 %copy-start.6 = (bf16[768,32]{0,1:T(8,128)(2,1)S(1)}, bf16[768,32]{0,1:T(8,128)(2,1)}, u32[]{:S(2)}) copy-start(bf16[768,32]{0,1:T(8,128)(2,1)} %param.21) | copy-start | bytes 147460
  563.5 324.6 %reduce-scatter.2.cloned.1.call-start = ((), (), s32[]{:S(2)}) async-start(), calls=%async_computation.4 | async-start | bytes 147456 | tf_op jit(solution)/shard_map/reduce_scatter | solution.py:70
Sparse Core Ops, SparseCore 0:
  273.1 274.0 all-reduce.2
  563.6 287.3 all-reduce.4
  854.0 33.9 reduce-scatter.1
